TPU v7x, 32 devices: a whole 2x2x4 slice. The times are simulated.
32 devices in a mesh: group: 2 (over x), tm: 16 (over z, y, core).
Axes of the slice: x: 2, y: 2, z: 4, core: 2. Of those that a mesh axis runs over, the one named last changes fastest.
Arguments:
- records: float32 [256, 262144], P('group', 'tm'), parts along dimension 0, may hold values from -6 to 6
- labels: int32 [256], P('group'), parts along dimension 0, may hold values from 0 to 1
- first_weight: bfloat16 [131072, 1024], P('tm'), may hold values from -0.015625 to 0.015625
- first_bias: float32 [1024], replicated, may hold values from -3 to 3
- second_weight: float32 [1024], replicated, may hold values from -0.1875 to 0.1875
- second_bias: float32 [1], replicated, may hold values from -3 to 3
Outputs:
- loss: float32 [2], P('group'), parts along dimension 0
- grad_first: float32 [262144, 1024], P(('group', 'tm')), parts along dimension 0
- grad_bias: float32 [2048], P('group'), parts along dimension 0
- grad_second: float32 [2048], P('group'), parts along dimension 0
- grad_out_bias: float32 [2], P('group'), parts along dimension 0
There are 2 independent parts, one for each index of `group`. A program takes and returns all parts, laid end to end along the dimension named above; an argument that names none is the same for every part. Nothing has to cross between parts.
All inputs are finite; a program needn't handle non-finite values.
Results may differ from a plain program's by a relative error of at most 0.0079.
Values may be sent and summed in bfloat16 or wider, within the bound.
No kernel may reach another device: no remote copies, remote signals or barrier semaphores. Data moves between devices by JAX's collectives and lax.ppermute only.
A program may use at most 192 MiB of HBM per device.

v0:
```python
import math
import jax
import jax.numpy as jnp
from jax import lax
from jax.sharding import PartitionSpec as P

N1 = 512
N2 = 512


def first_table(count):
    rows = jnp.arange(count, dtype=jnp.int32)[:, None]
    cols = jnp.arange(count, dtype=jnp.int32)[None, :]
    angle = 2.0 * math.pi / count * (rows * cols % count).astype(jnp.float32)
    scale = 1.0 / math.sqrt(count)
    return jnp.concatenate([jnp.cos(angle) * scale, -jnp.sin(angle) * scale], 0).astype(
        jnp.bfloat16
    )


def second_table(count):
    rows = jnp.arange(count, dtype=jnp.int32)[:, None]
    cols = jnp.arange(count // 2, dtype=jnp.int32)[None, :]
    angle = 2.0 * math.pi / count * (rows * cols % count).astype(jnp.float32)
    scale = 1.0 / math.sqrt(count)
    cosine = jnp.cos(angle) * scale
    sine = jnp.sin(angle) * scale
    upper = jnp.concatenate([cosine, -sine], 1)
    lower = jnp.concatenate([sine, cosine], 1)
    return jnp.concatenate([upper, lower], 0).astype(jnp.bfloat16)


def on_device(records, labels, first_weight, first_bias, second_weight, second_bias):
    devices = lax.axis_size("tm")
    slow_rows = N2 // devices
    fast_cols = N1 // devices
    table_one = first_table(N2)
    table_two = second_table(N1)
    total_len = N1 * N2
    count_rec = records.shape[0]
    samples = records.astype(jnp.bfloat16).reshape(count_rec, slow_rows, N1)
    samples = jnp.transpose(samples, (0, 2, 1))
    partial_value = jnp.einsum(
        "rcn,kn->rck",
        lax.all_to_all(samples, "tm", split_axis=1, concat_axis=2, tiled=True),
        table_one,
        preferred_element_type=jnp.float32,
    )
    real_part = partial_value[:, :, :N2]
    imag_part = partial_value[:, :, N2:]
    fast = lax.axis_index("tm") * fast_cols + jnp.arange(fast_cols, dtype=jnp.int32)
    slow = jnp.arange(N2, dtype=jnp.int32)
    phase = (
        2.0 * math.pi / total_len * (fast[:, None] * slow[None, :] % total_len).astype(jnp.float32)
    )
    cosine = jnp.cos(phase)[None]
    sine = jnp.sin(phase)[None]
    twisted_re = real_part * cosine + imag_part * sine
    twisted_im = imag_part * cosine - real_part * sine
    stacked = jnp.stack([twisted_re, twisted_im], 1).astype(jnp.bfloat16)
    twisted = jnp.transpose(stacked, (0, 3, 1, 2))
    block = lax.all_to_all(twisted, "tm", split_axis=1, concat_axis=3, tiled=True)
    count = block.shape[0]
    joined = block.reshape(count, block.shape[1], 2 * N1)
    bins = jnp.einsum("rbm,mf->rbf", joined, table_two, preferred_element_type=jnp.float32)
    power = bins[:, :, : N1 // 2] ** 2 + bins[:, :, N1 // 2 :] ** 2
    features = jnp.log(1.0 + power).astype(jnp.bfloat16).reshape(count, block.shape[1] * (N1 // 2))
    target = labels.astype(jnp.float32)
    partial_sums = jnp.dot(features, first_weight, preferred_element_type=jnp.float32)
    pre = lax.psum(partial_sums, "tm") + first_bias[None, :]
    gate = jax.nn.sigmoid(pre)
    hidden = pre * gate
    logit = jnp.sum(hidden * second_weight[None, :], 1) + second_bias[0]
    dlogit = jax.nn.sigmoid(logit) - target
    dpre = (dlogit[:, None] * second_weight[None, :] * gate * (1.0 + pre * (1.0 - gate))).astype(
        jnp.bfloat16
    )
    grad_first = lax.dot_general(
        features, dpre, (((0,), (0,)), ((), ())), preferred_element_type=jnp.float32
    )
    grad_bias = jnp.sum(dpre.astype(jnp.float32), 0)
    grad_second = jnp.sum(hidden * dlogit[:, None], 0)
    loss = jnp.mean(jnp.log(1.0 + jnp.exp(logit)) - target * logit).reshape(1)
    grad_out_bias = jnp.sum(dlogit).reshape(1)
    return (loss, grad_first, grad_bias, grad_second, grad_out_bias)


def solution(mesh):
    return jax.shard_map(
        on_device,
        mesh=mesh,
        in_specs=(P("group", "tm"), P("group"), P("tm", None), P(), P(), P()),
        out_specs=(P("group"), P(("group", "tm"), None), P("group"), P("group"), P("group")),
        check_vma=False,
    )
```

profile of v0, /device:TPU:1, one launch (start us, length us, event | category | flops | bytes accessed | tf_op | source)
XLA Modules:
  0.0 488.0 jit_solution(15323579355672855773)
XLA Ops:
  7.2 7.2 %copy.31 = bf16[128,16384]{0,1:T(8,128)(2,1)} copy(f32[128,16384]{1,0:T(8,128)} %param.6) | data formatting | bytes 12582912 | tf_op args[0]
  14.4 6.9 %copy.32 = bf16[128,512,32]{0,2,1:T(8,128)(2,1)} copy(bf16[128,512,32]{0,1,2:T(8,128)(2,1)} %bitcast.39) | data formatting | bytes 8388608 | tf_op jit(solution)/shard_map/transpose | solution.py:42
  21.2 7.3 %all-to-all-start = ((bf16[128,512,32]{0,2,1:T(8,128)(2,1)}), bf16[128,512,32]{0,2,1:T(8,128)(2,1)}, u32[]{:S(2)}, u32[]{:S(2)}) async-start(bf16[128,512,32]{0,2,1:T(8,128)(2,1)} %copy.32), calls=%async_computation | async-start | bytes 8388608 | tf_op jit(solution)/shard_map/all_to_all | solution.py:45
  28.6 4.4 multiply_convert_fusion
  33.0 0.3 fusion.36
  33.3 73.3 %all-to-all-done = bf16[128,512,32]{0,2,1:T(8,128)(2,1)} async-done(((bf16[128,512,32]{0,2,1:T(8,128)(2,1)}), bf16[128,512,32]{0,2,1:T(8,128)(2,1)}, u32[]{:S(2)}, u32[]{:S(2)}) %all-to-all-start) | async-done | bytes 4194336 | tf_op jit(solution)/shard_map/all_to_all | solution.py:45
  106.7 3.4 copy.33
  110.1 4.5 convolution_bitcast_fusion
  114.7 5.8 %fusion = (bf16[128,1,32,512]{0,3,2,1:T(8,128)(2,1)S(1)}, bf16[128,1,32,512]{0,3,2,1:T(8,128)(2,1)}) fusion(f32[128,32,1024]{0,2,1:T(8,128)S(1)} %convolution_bitcast_fusion, f32[32,512]{1,0:T(8,128)S(1)} %get-tuple-element.14, f32[32,512]{1,0:T(8,128)S(1)} %get-tuple-element.13), kind=kLoop, calls=%fused_computation.4 | loop fusion | flops 16777216 | bytes 25296896 | tf_op jit(solution)/shard_map/stack | solution.py:60
  120.5 6.3 %maximum_bitcast_fusion = bf16[128,512,2,32]{0,1,3,2:T(8,128)(2,1)} fusion(bf16[128,1,32,512]{0,3,2,1:T(8,128)(2,1)} %get-tuple-element.10, bf16[128,1,32,512]{0,3,2,1:T(8,128)(2,1)S(1)} %get-tuple-element.9), kind=kLoop, calls=%fused_computation.1 | loop fusion | flops 4194304 | bytes 16777216 | tf_op jit(solution)/shard_map/transpose | solution.py:61
  126.8 12.0 %copy.35 = bf16[128,512,2,32]{0,3,2,1:T(8,128)(2,1)} copy(bf16[128,512,2,32]{0,1,3,2:T(8,128)(2,1)} %maximum_bitcast_fusion) | data formatting | bytes 16777216 | tf_op jit(solution)/shard_map/transpose | solution.py:61
  138.8 19.3 %all-to-all-start.1 = ((bf16[128,512,2,32]{0,3,2,1:T(8,128)(2,1)}), bf16[128,512,2,32]{0,3,2,1:T(8,128)(2,1)}, u32[]{:S(2)}, u32[]{:S(2)}) async-start(bf16[128,512,2,32]{0,3,2,1:T(8,128)(2,1)} %copy.35), calls=%async_computation.1 | async-start | bytes 16777216 | tf_op jit(solution)/shard_map/all_to_all | solution.py:62
  158.1 0.0 all-reduce.2.cloned.1.call-start
  158.2 2.2 fusion.28
  160.4 2.2 negate_convert_fusion
  162.6 146.6 %all-to-all-done.1 = bf16[128,512,2,32]{0,3,2,1:T(8,128)(2,1)} async-done(((bf16[128,512,2,32]{0,3,2,1:T(8,128)(2,1)}), bf16[128,512,2,32]{0,3,2,1:T(8,128)(2,1)}, u32[]{:S(2)}, u32[]{:S(2)}) %all-to-all-start.1) | async-done | bytes 8388640 | tf_op jit(solution)/shard_map/all_to_all | solution.py:62
  309.2 9.0 %copy.36 = bf16[128,32,2,16,32]{0,4,3,2,1:T(8,128)(2,1)} copy(bf16[128,32,2,16,32]{0,4,2,1,3:T(8,128)(2,1)} %bitcast.11) | data formatting | bytes 16777216 | tf_op jit(solution)/shard_map/all_to_all | solution.py:62
  318.2 7.0 %fusion.11 = f32[128,32,512]{2,0,1:T(8,128)S(1)} fusion(bf16[128,32,1024]{0,2,1:T(8,128)(2,1)} %bitcast.36, bf16[512,256]{1,0:T(8,128)(2,1)S(1)} %get-tuple-element.18, bf16[512,256]{1,0:T(8,128)(2,1)S(1)} %fusion.28, bf16[512,256]{1,0:T(8,128)(2,1)S(1)} %get-tuple-element.17), kind=kOutput, calls=%fused_computation.22 | convolution fusion | flops 4299161600 | bytes 17563648 | tf_op jit(solution)/shard_map/rbm,mf->rbf/dot_general | solution.py:65
  325.2 2.3 fusion.5
  327.5 3.2 copy.38
  330.7 0.0 copy-start
  330.7 0.0 copy-start.1
  330.7 0.0 copy-start.2
  330.7 8.9 %fusion.40 = f32[128,1024]{1,0:T(8,128)} fusion(bf16[128,8192]{0,1:T(8,128)(2,1)S(1)} %bitcast.37, bf16[8192,1024]{1,0:T(8,128)(2,1)} %param.8), kind=kOutput, calls=%fused_computation.70 | convolution fusion | flops 2147483648 | bytes 19398656 | tf_op jit(solution)/shard_map/dot_general | solution.py:69
  339.7 0.0 all-reduce.2.cloned.1.call-update
  340.3 121.1 %all-reduce.2.cloned.1.call-done = f32[128,1024]{1,0:T(8,128)} async-done(((f32[128,1024]{1,0:T(8,128)}), f32[128,1024]{1,0:T(8,128)}) %all-reduce.2.cloned.1.call-update) | async-done | bytes 524304 | tf_op jit(solution)/shard_map/psum | solution.py:70
  461.4 0.0 copy-done
  461.4 0.0 copy-done.1
  461.4 1.3 multiply_reduce_fusion.1
  462.7 0.7 fusion.39
  463.4 1.9 convert_reduce_fusion
  465.4 14.0 %fusion.41 = f32[8192,1024]{1,0:T(8,128)} fusion(bf16[128,8192]{0,1:T(8,128)(2,1)S(1)} %bitcast.38, bf16[128,1024]{1,0:T(8,128)(2,1)S(1)} %get-tuple-element.8), kind=kOutput, calls=%fused_computation.71 | convolution fusion | flops 2147483648 | bytes 35913728 | tf_op jit(solution)/shard_map/dot_general | solution.py:78
  (2 shorter events, 0.0 us)
Async XLA Ops:
  21.2 85.4 %all-to-all-start = ((bf16[128,512,32]{0,2,1:T(8,128)(2,1)}), bf16[128,512,32]{0,2,1:T(8,128)(2,1)}, u32[]{:S(2)}, u32[]{:S(2)}) async-start(bf16[128,512,32]{0,2,1:T(8,128)(2,1)} %copy.32), calls=%async_computation | async-start | bytes 8388608 | tf_op jit(solution)/shard_map/all_to_all | solution.py:45
  138.8 170.4 %all-to-all-start.1 = ((bf16[128,512,2,32]{0,3,2,1:T(8,128)(2,1)}), bf16[128,512,2,32]{0,3,2,1:T(8,128)(2,1)}, u32[]{:S(2)}, u32[]{:S(2)}) async-start(bf16[128,512,2,32]{0,3,2,1:T(8,128)(2,1)} %copy.35), calls=%async_computation.1 | async-start | bytes 16777216 | tf_op jit(solution)/shard_map/all_to_all | solution.py:62
  158.1 303.3 %all-reduce.2.cloned.1.call-start = ((), (), s32[]{:S(2)}) async-start(), calls=%async_computation.2 | async-start | bytes 1048576 | tf_op jit(solution)/shard_map/psum | solution.py:70
  330.7 130.7 %copy-start = (f32[1024]{0:T(1024)S(1)}, f32[1024]{0:T(1024)}, u32[]{:S(2)}) copy-start(f32[1024]{0:T(1024)} %param.10) | copy-start | bytes 12292
  330.7 130.7 %copy-start.1 = (f32[1024]{0:T(1024)S(1)}, f32[1024]{0:T(1024)}, u32[]{:S(2)}) copy-start(f32[1024]{0:T(1024)} %param.9) | copy-start | bytes 12292
  330.7 132.0 %copy-start.2 = (s32[128]{0:T(128)S(1)}, s32[128]{0:T(128)}, u32[]{:S(2)}) copy-start(s32[128]{0:T(128)} %param.7) | copy-start | bytes 1540
Sparse Core Ops, SparseCore 0:
  339.8 121.5 all-reduce.1
where the time goes:
time: 489 us; the launch traced here: 488 us
  waiting for transfers between devices  341 us (70%)
  local copies, waits for them, and re-layouts  41.7 us (9%)
  matrix products  34.5 us (7%)
  other arithmetic  27.5 us (6%)
  starting transfers between devices  26.7 us (5%)
  between operations  16.6 us (3%)
    all_to_all x1, waiting for transfers between devices, on_device(): lax.all_to_all(twisted, 'tm', split_axis=1, concat_axis=3, tiled=True)  147 us
    psum x1, waiting for transfers between devices, on_device(): pre = lax.psum(partial_sums, 'tm') + first_bias[None, :]  121 us
    all_to_all x1, waiting for transfers between devices, on_device(): lax.all_to_all(samples, 'tm', split_axis=1, concat_axis=2, tiled=True)  73.3 us
    all_to_all x1, starting transfers between devices, on_device(): lax.all_to_all(twisted, 'tm', split_axis=1, concat_axis=3, tiled=True)  19.3 us
    dot_general x1, matrix products, on_device(): lax.dot_general(features, dpre, (((0,), (0,)), ((), ())), preferred_eleme...  14 us
    transpose x1, local copies, waits for them, and re-layouts, on_device(): twisted = jnp.transpose(stacked, (0, 3, 1, 2))  12 us
  transfers between devices with their start and end apart: 3, of which 3 were waited for; matrix products, arithmetic and copies ran while one was open for 2% of the time, Pallas kernels for 0%

commit v1 on v0

--- a/solution.py
+++ b/solution.py
@@ -6,6 +6,18 @@
 
 N1 = 512
 N2 = 512
+
+
+def in_blocks(x, dim, length):
+    shape = x.shape
+    blocks = x.reshape(*shape[:dim], length, shape[dim] // length, *shape[dim + 1 :])
+    return jnp.moveaxis(blocks, dim, 0)
+
+
+def joined_along(tiles, dim):
+    tiles = jnp.moveaxis(tiles, 0, dim)
+    lengths = tiles.shape
+    return tiles.reshape(*lengths[:dim], lengths[dim] * lengths[dim + 1], *lengths[dim + 2 :])
 
 
 def first_table(count):
@@ -59,7 +71,14 @@
     twisted_im = imag_part * cosine - real_part * sine
     stacked = jnp.stack([twisted_re, twisted_im], 1).astype(jnp.bfloat16)
     twisted = jnp.transpose(stacked, (0, 3, 1, 2))
-    block = lax.all_to_all(twisted, "tm", split_axis=1, concat_axis=3, tiled=True)
+    devices_2, place = (lax.axis_size("tm"), lax.axis_index("tm"))
+    parts = in_blocks(twisted, 1, devices_2)
+    outs = [parts[place]]
+    for step in range(1, devices_2):
+        sent = parts[place ^ step]
+        outs.append(lax.ppermute(sent, "tm", [(i, i ^ step) for i in range(devices_2)]))
+    parts = jnp.stack(outs)[place ^ jnp.arange(devices_2)]
+    block = joined_along(parts, 3)
     count = block.shape[0]
     joined = block.reshape(count, block.shape[1], 2 * N1)
     bins = jnp.einsum("rbm,mf->rbf", joined, table_two, preferred_element_type=jnp.float32)

time: 489 us -> 515 us (1.053)
  starting transfers between devices: 26.7 us -> 103 us
  waiting for transfers between devices: 341 us -> 273 us
  local copies, waits for them, and re-layouts: 41.7 us -> 59.7 us
    all_to_all x1 -> x0, waiting for transfers between devices: 147 us -> none  [on_device(): lax.all_to_all(twisted, 'tm', split_axis=1, concat_axis=3, tiled=True)]
    ppermute x0 -> x15, starting transfers between devices: none -> 95.2 us  [on_device(): lax.ppermute(sent, 'tm', [(i, i ^ step) for i in range(devices_2)])]
    ppermute x0 -> x15, waiting for transfers between devices: none -> 71.1 us  [on_device(): lax.ppermute(sent, 'tm', [(i, i ^ step) for i in range(devices_2)])]
    all_to_all x1 -> x0, starting transfers between devices: 19.3 us -> none  [on_device(): lax.all_to_all(twisted, 'tm', split_axis=1, concat_axis=3, tiled=True)]
    unnamed x7 -> x22, local copies, waits for them, and re-layouts: 7.25 us -> 19.8 us
    psum x1, waiting for transfers between devices: 121 us -> 131 us  [on_device(): pre = lax.psum(partial_sums, 'tm') + first_bias[None, :]]
    all_to_all x1 -> x0, local copies, waits for them, and re-layouts: 8.97 us -> none  [on_device(): lax.all_to_all(twisted, 'tm', split_axis=1, concat_axis=3, tiled=True)]
    another operation x0 -> x17, local copies, waits for them, and re-layouts: none -> 8.96 us
  transfers between devices with their start and end apart: 3 -> 17, of which waited for: 3 -> 6; matrix products, arithmetic and copies ran while one was open for 2% -> 5% of each run, Pallas kernels for 0% -> 0%
where the time goes in v1:
time: 515 us; the launch traced here: 514 us
  waiting for transfers between devices  273 us (53%)
  starting transfers between devices  103 us (20%)
  local copies, waits for them, and re-layouts  59.7 us (12%)
  matrix products  34.5 us (7%)
  other arithmetic  27.5 us (5%)
  between operations  16.8 us (3%)
    psum x1, waiting for transfers between devices, on_device(): pre = lax.psum(partial_sums, 'tm') + first_bias[None, :]  131 us
    ppermute x15, starting transfers between devices, on_device(): lax.ppermute(sent, 'tm', [(i, i ^ step) for i in range(devices_2)])  95.2 us
    ppermute x15, waiting for transfers between devices, on_device(): lax.ppermute(sent, 'tm', [(i, i ^ step) for i in range(devices_2)])  71.1 us
    all_to_all x1, waiting for transfers between devices, on_device(): lax.all_to_all(samples, 'tm', split_axis=1, concat_axis=2, tiled=True)  71 us
    unnamed x22, local copies, waits for them, and re-layouts  19.8 us
    dot_general x1, matrix products, on_device(): lax.dot_general(features, dpre, (((0,), (0,)), ((), ())), preferred_eleme...  14 us
    another operation x2, other arithmetic, on_device(): stacked = jnp.stack([twisted_re, twisted_im], 1).astype(jnp.bfloat16)  12.2 us
  transfers between devices with their start and end apart: 17, of which 6 were waited for; matrix products, arithmetic and copies ran while one was open for 5% of the time, Pallas kernels for 0%

profile of v1, /device:TPU:1, one launch (start us, length us, event | category | flops | bytes accessed | tf_op | source)
XLA Modules:
  0.0 513.9 jit_solution(34020048407920911)
XLA Ops:
  7.2 7.2 %copy.55 = bf16[128,16384]{0,1:T(8,128)(2,1)} copy(f32[128,16384]{1,0:T(8,128)} %param.6) | data formatting | bytes 12582912 | tf_op args[0]
  14.4 6.8 %copy.56 = bf16[128,512,32]{0,2,1:T(8,128)(2,1)} copy(bf16[128,512,32]{0,1,2:T(8,128)(2,1)} %bitcast.119) | data formatting | bytes 8388608 | tf_op jit(solution)/shard_map/transpose | solution.py:54
  21.2 7.3 %all-to-all-start = ((bf16[128,512,32]{0,2,1:T(8,128)(2,1)}), bf16[128,512,32]{0,2,1:T(8,128)(2,1)}, u32[]{:S(2)}, u32[]{:S(2)}) async-start(bf16[128,512,32]{0,2,1:T(8,128)(2,1)} %copy.56), calls=%async_computation | async-start | bytes 8388608 | tf_op jit(solution)/shard_map/all_to_all | solution.py:57
  30.9 4.4 multiply_convert_fusion
  35.7 71.0 %all-to-all-done = bf16[128,512,32]{0,2,1:T(8,128)(2,1)} async-done(((bf16[128,512,32]{0,2,1:T(8,128)(2,1)}), bf16[128,512,32]{0,2,1:T(8,128)(2,1)}, u32[]{:S(2)}, u32[]{:S(2)}) %all-to-all-start) | async-done | bytes 4194336 | tf_op jit(solution)/shard_map/all_to_all | solution.py:57
  106.7 3.4 copy.57
  110.1 4.5 convolution_bitcast_fusion
  114.6 5.8 %fusion = (bf16[128,1,32,512]{0,3,2,1:T(8,128)(2,1)S(1)}, bf16[128,1,32,512]{0,3,2,1:T(8,128)(2,1)}) fusion(f32[128,32,1024]{0,2,1:T(8,128)S(1)} %convolution_bitcast_fusion, f32[32,512]{1,0:T(8,128)S(1)} %get-tuple-element.30, f32[32,512]{1,0:T(8,128)S(1)} %get-tuple-element.29), kind=kLoop, calls=%fused_computation.5 | loop fusion | flops 16777216 | bytes 25296896 | tf_op jit(solution)/shard_map/stack | solution.py:72
  120.5 6.3 %pad_maximum_fusion = bf16[128,2,32,512]{0,3,2,1:T(8,128)(2,1)} fusion(bf16[128,1,32,512]{0,3,2,1:T(8,128)(2,1)} %get-tuple-element.10, bf16[128,1,32,512]{0,3,2,1:T(8,128)(2,1)S(1)} %get-tuple-element.9), kind=kLoop, calls=%fused_computation.2 | loop fusion | flops 4194304 | bytes 16777216 | tf_op jit(solution)/shard_map/stack | solution.py:72
  126.8 5.0 constant_dynamic-slice_fusion
  132.2 2.4 negate_convert_fusion
  134.8 6.0 %collective-permute-start.1 = (bf16[128,32,2,32]{0,3,2,1:T(8,128)(2,1)S(1)}, bf16[128,32,2,32]{0,3,2,1:T(8,128)(2,1)S(1)}, u32[]{:S(2)}, u32[]{:S(2)}) collective-permute-start(bf16[128,32,2,32]{0,3,2,1:T(8,128)(2,1)S(1)} %bitcast.133), channel_id=1, source_target_pairs={{0,2},{1,3},{2,0},{3,1},{4,6},{5,7},{6,4},{7,5},{8,10},{9,11},{10,... | collective-permute-start | bytes 1572872 | tf_op jit(solution)/shard_map/ppermute | solution.py:79
  141.9 11.0 %collective-permute-start.3 = (bf16[128,32,2,32]{0,3,2,1:T(8,128)(2,1)S(1)}, bf16[128,32,2,32]{0,3,2,1:T(8,128)(2,1)S(1)}, u32[]{:S(2)}, u32[]{:S(2)}) collective-permute-start(bf16[128,32,2,32]{0,3,2,1:T(8,128)(2,1)S(1)} %bitcast.130), channel_id=1, source_target_pairs={{0,4},{1,5},{2,6},{3,7},{4,0},{5,1},{6,2},{7,3},{8,12},{9,13},{10,... | collective-permute-start | bytes 1572872 | tf_op jit(solution)/shard_map/ppermute | solution.py:79
  156.5 2.7 collective-permute-start.5
  160.0 6.7 %collective-permute-start.6 = (bf16[128,32,2,32]{0,3,2,1:T(8,128)(2,1)S(1)}, bf16[128,32,2,32]{0,3,2,1:T(8,128)(2,1)S(1)}, u32[]{:S(2)}, u32[]{:S(2)}) collective-permute-start(bf16[128,32,2,32]{0,3,2,1:T(8,128)(2,1)S(1)} %bitcast.131), channel_id=1, source_target_pairs={{0,7},{1,6},{2,5},{3,4},{4,3},{5,2},{6,1},{7,0},{8,15},{9,14},{10,... | collective-permute-start | bytes 1572872 | tf_op jit(solution)/shard_map/ppermute | solution.py:79
  167.5 9.8 %collective-permute-start.7 = (bf16[128,32,2,32]{0,3,2,1:T(8,128)(2,1)S(1)}, bf16[128,32,2,32]{0,3,2,1:T(8,128)(2,1)S(1)}, u32[]{:S(2)}, u32[]{:S(2)}) collective-permute-start(bf16[128,32,2,32]{0,3,2,1:T(8,128)(2,1)S(1)} %bitcast.129), channel_id=1, source_target_pairs={{0,8},{1,9},{2,10},{3,11},{4,12},{5,13},{6,14},{7,15},{8,0},{9,1},... | collective-permute-start | bytes 1572872 | tf_op jit(solution)/shard_map/ppermute | solution.py:79
  179.0 2.4 collective-permute-start.9
  182.2 30.2 %collective-permute-done.5 = bf16[128,32,2,32]{0,3,2,1:T(8,128)(2,1)S(1)} collective-permute-done((bf16[128,32,2,32]{0,3,2,1:T(8,128)(2,1)S(1)}, bf16[128,32,2,32]{0,3,2,1:T(8,128)(2,1)S(1)}, u32[]{:S(2)}, u32[]{:S(2)}) %collective-permute-start.5) | collective-permute-done | bytes 524320 | tf_op jit(solution)/shard_map/ppermute | solution.py:79
  213.6 10.2 %collective-permute-done.6 = bf16[128,32,2,32]{0,3,2,1:T(8,128)(2,1)S(1)} collective-permute-done((bf16[128,32,2,32]{0,3,2,1:T(8,128)(2,1)S(1)}, bf16[128,32,2,32]{0,3,2,1:T(8,128)(2,1)S(1)}, u32[]{:S(2)}, u32[]{:S(2)}) %collective-permute-start.6) | collective-permute-done | bytes 524320 | tf_op jit(solution)/shard_map/ppermute | solution.py:79
  225.9 2.4 collective-permute-start.12
  229.2 47.9 %collective-permute-start.13 = (bf16[128,32,2,32]{0,3,2,1:T(8,128)(2,1)S(1)}, bf16[128,32,2,32]{0,3,2,1:T(8,128)(2,1)S(1)}, u32[]{:S(2)}, u32[]{:S(2)}) collective-permute-start(bf16[128,32,2,32]{0,3,2,1:T(8,128)(2,1)S(1)} %bitcast.122), channel_id=1, source_target_pairs={{0,14},{1,15},{2,12},{3,13},{4,10},{5,11},{6,8},{7,9},{8,6},{9,7},... | collective-permute-start | bytes 1572872 | tf_op jit(solution)/shard_map/ppermute | solution.py:79
  277.9 12.5 %collective-permute-done.9 = bf16[128,32,2,32]{0,3,2,1:T(8,128)(2,1)S(1)} collective-permute-done((bf16[128,32,2,32]{0,3,2,1:T(8,128)(2,1)S(1)}, bf16[128,32,2,32]{0,3,2,1:T(8,128)(2,1)S(1)}, u32[]{:S(2)}, u32[]{:S(2)}) %collective-permute-start.9) | collective-permute-done | bytes 524320 | tf_op jit(solution)/shard_map/ppermute | solution.py:79
  290.4 3.7 collective-permute-start.14
  295.0 18.1 %collective-permute-done.10 = bf16[128,32,2,32]{0,3,2,1:T(8,128)(2,1)S(1)} collective-permute-done((bf16[128,32,2,32]{0,3,2,1:T(8,128)(2,1)S(1)}, bf16[128,32,2,32]{0,3,2,1:T(8,128)(2,1)S(1)}, u32[]{:S(2)}, u32[]{:S(2)}) %collective-permute-start.10) | collective-permute-done | bytes 524320 | tf_op jit(solution)/shard_map/ppermute | solution.py:79
  317.3 8.1 %gather_fusion = bf16[16,128,32,2,32]{1,4,3,2,0:T(8,128)(2,1)} fusion(bf16[16,128,32,2,32]{1,4,3,2,0:T(8,128)(2,1)} %bitcast_dynamic-update-slice_fusion, s32[1024]{0:T(1024)S(1)} %pad_clamp_fusion), kind=kCustom, calls=%fused_computation | custom fusion | bytes 16777280 | tf_op jit(solution)/shard_map/gather | solution.py:80
  325.4 9.0 %copy.75 = bf16[128,32,2,16,32]{0,4,3,2,1:T(8,128)(2,1)} copy(bf16[128,32,2,16,32]{0,4,2,1,3:T(8,128)(2,1)} %bitcast.114) | data formatting | bytes 16777216 | tf_op jit(solution)/shard_map/transpose | solution.py:18
  334.4 7.0 %fusion.11 = f32[128,32,512]{2,0,1:T(8,128)S(1)} fusion(bf16[128,32,1024]{0,2,1:T(8,128)(2,1)} %bitcast.115, bf16[512,256]{1,0:T(8,128)(2,1)S(1)} %get-tuple-element.34, bf16[512,256]{1,0:T(8,128)(2,1)S(1)} %fusion.28, bf16[512,256]{1,0:T(8,128)(2,1)S(1)} %get-tuple-element.33), kind=kOutput, calls=%fused_computation.23 | convolution fusion | flops 4299161600 | bytes 17563648 | tf_op jit(solution)/shard_map/rbm,mf->rbf/dot_general | solution.py:84
  341.4 2.3 fusion.5
  343.7 3.5 copy.77
  347.2 8.9 %fusion.41 = f32[128,1024]{1,0:T(8,128)} fusion(bf16[128,8192]{0,1:T(8,128)(2,1)S(1)} %bitcast.117, bf16[8192,1024]{1,0:T(8,128)(2,1)} %param.8), kind=kOutput, calls=%fused_computation.121 | convolution fusion | flops 2147483648 | bytes 19398656 | tf_op jit(solution)/shard_map/dot_general | solution.py:88
  356.8 130.6 %all-reduce.2.cloned.1.call-done = f32[128,1024]{1,0:T(8,128)} async-done(((f32[128,1024]{1,0:T(8,128)}), f32[128,1024]{1,0:T(8,128)}) %all-reduce.2.cloned.1.call-update) | async-done | bytes 524304 | tf_op jit(solution)/shard_map/psum | solution.py:89
  491.3 14.0 %fusion.42 = f32[8192,1024]{1,0:T(8,128)} fusion(bf16[128,8192]{0,1:T(8,128)(2,1)S(1)} %bitcast.118, bf16[128,1024]{1,0:T(8,128)(2,1)S(1)} %get-tuple-element.8), kind=kOutput, calls=%fused_computation.122 | convolution fusion | flops 2147483648 | bytes 35913728 | tf_op jit(solution)/shard_map/dot_general | solution.py:97
  (64 shorter events, 25.6 us)
Async XLA Ops:
  21.2 85.4 %all-to-all-start = ((bf16[128,512,32]{0,2,1:T(8,128)(2,1)}), bf16[128,512,32]{0,2,1:T(8,128)(2,1)}, u32[]{:S(2)}, u32[]{:S(2)}) async-start(bf16[128,512,32]{0,2,1:T(8,128)(2,1)} %copy.56), calls=%async_computation | async-start | bytes 8388608 | tf_op jit(solution)/shard_map/all_to_all | solution.py:57
  28.6 458.8 %all-reduce.2.cloned.1.call-start = ((), (), s32[]{:S(2)}) async-start(), calls=%async_computation.1 | async-start | bytes 1048576 | tf_op jit(solution)/shard_map/psum | solution.py:89
  132.1 24.4 %collective-permute-start = (bf16[128,32,2,32]{0,3,2,1:T(8,128)(2,1)S(1)}, bf16[128,32,2,32]{0,3,2,1:T(8,128)(2,1)S(1)}, u32[]{:S(2)}, u32[]{:S(2)}) collective-permute-start(bf16[128,32,2,32]{0,3,2,1:T(8,128)(2,1)S(1)} %bitcast.132), channel_id=1, source_target_pairs={{0,1},{1,0},{2,3},{3,2},{4,5},{5,4},{6,7},{7,6},{8,9},{9,8},{10,11... | collective-permute-start | bytes 1572872 | tf_op jit(solution)/shard_map/ppermute | solution.py:79
  134.8 25.2 %collective-permute-start.1 = (bf16[128,32,2,32]{0,3,2,1:T(8,128)(2,1)S(1)}, bf16[128,32,2,32]{0,3,2,1:T(8,128)(2,1)S(1)}, u32[]{:S(2)}, u32[]{:S(2)}) collective-permute-start(bf16[128,32,2,32]{0,3,2,1:T(8,128)(2,1)S(1)} %bitcast.133), channel_id=1, source_target_pairs={{0,2},{1,3},{2,0},{3,1},{4,6},{5,7},{6,4},{7,5},{8,10},{9,11},{10,... | collective-permute-start | bytes 1572872 | tf_op jit(solution)/shard_map/ppermute | solution.py:79
  141.4 26.1 %collective-permute-start.2 = (bf16[128,32,2,32]{0,3,2,1:T(8,128)(2,1)S(1)}, bf16[128,32,2,32]{0,3,2,1:T(8,128)(2,1)S(1)}, u32[]{:S(2)}, u32[]{:S(2)}) collective-permute-start(bf16[128,32,2,32]{0,3,2,1:T(8,128)(2,1)S(1)} %bitcast.134), channel_id=1, source_target_pairs={{0,3},{1,2},{2,1},{3,0},{4,7},{5,6},{6,5},{7,4},{8,11},{9,10},{10,... | collective-permute-start | bytes 1572872 | tf_op jit(solution)/shard_map/ppermute | solution.py:79
  141.9 36.2 %collective-permute-start.3 = (bf16[128,32,2,32]{0,3,2,1:T(8,128)(2,1)S(1)}, bf16[128,32,2,32]{0,3,2,1:T(8,128)(2,1)S(1)}, u32[]{:S(2)}, u32[]{:S(2)}) collective-permute-start(bf16[128,32,2,32]{0,3,2,1:T(8,128)(2,1)S(1)} %bitcast.130), channel_id=1, source_target_pairs={{0,4},{1,5},{2,6},{3,7},{4,0},{5,1},{6,2},{7,3},{8,12},{9,13},{10,... | collective-permute-start | bytes 1572872 | tf_op jit(solution)/shard_map/ppermute | solution.py:79
  152.9 26.0 %collective-permute-start.4 = (bf16[128,32,2,32]{0,3,2,1:T(8,128)(2,1)S(1)}, bf16[128,32,2,32]{0,3,2,1:T(8,128)(2,1)S(1)}, u32[]{:S(2)}, u32[]{:S(2)}) collective-permute-start(bf16[128,32,2,32]{0,3,2,1:T(8,128)(2,1)S(1)} %bitcast.128), channel_id=1, source_target_pairs={{0,5},{1,4},{2,7},{3,6},{4,1},{5,0},{6,3},{7,2},{8,13},{9,12},{10,... | collective-permute-start | bytes 1572872 | tf_op jit(solution)/shard_map/ppermute | solution.py:79
  156.5 56.0 %collective-permute-start.5 = (bf16[128,32,2,32]{0,3,2,1:T(8,128)(2,1)S(1)}, bf16[128,32,2,32]{0,3,2,1:T(8,128)(2,1)S(1)}, u32[]{:S(2)}, u32[]{:S(2)}) collective-permute-start(bf16[128,32,2,32]{0,3,2,1:T(8,128)(2,1)S(1)} %bitcast.135), channel_id=1, source_target_pairs={{0,6},{1,7},{2,4},{3,5},{4,2},{5,3},{6,0},{7,1},{8,14},{9,15},{10,... | collective-permute-start | bytes 1572872 | tf_op jit(solution)/shard_map/ppermute | solution.py:79
  160.0 63.8 %collective-permute-start.6 = (bf16[128,32,2,32]{0,3,2,1:T(8,128)(2,1)S(1)}, bf16[128,32,2,32]{0,3,2,1:T(8,128)(2,1)S(1)}, u32[]{:S(2)}, u32[]{:S(2)}) collective-permute-start(bf16[128,32,2,32]{0,3,2,1:T(8,128)(2,1)S(1)} %bitcast.131), channel_id=1, source_target_pairs={{0,7},{1,6},{2,5},{3,4},{4,3},{5,2},{6,1},{7,0},{8,15},{9,14},{10,... | collective-permute-start | bytes 1572872 | tf_op jit(solution)/shard_map/ppermute | solution.py:79
  167.5 58.4 %collective-permute-start.7 = (bf16[128,32,2,32]{0,3,2,1:T(8,128)(2,1)S(1)}, bf16[128,32,2,32]{0,3,2,1:T(8,128)(2,1)S(1)}, u32[]{:S(2)}, u32[]{:S(2)}) collective-permute-start(bf16[128,32,2,32]{0,3,2,1:T(8,128)(2,1)S(1)} %bitcast.129), channel_id=1, source_target_pairs={{0,8},{1,9},{2,10},{3,11},{4,12},{5,13},{6,14},{7,15},{8,0},{9,1},... | collective-permute-start | bytes 1572872 | tf_op jit(solution)/shard_map/ppermute | solution.py:79
  178.1 51.0 %collective-permute-start.8 = (bf16[128,32,2,32]{0,3,2,1:T(8,128)(2,1)S(1)}, bf16[128,32,2,32]{0,3,2,1:T(8,128)(2,1)S(1)}, u32[]{:S(2)}, u32[]{:S(2)}) collective-permute-start(bf16[128,32,2,32]{0,3,2,1:T(8,128)(2,1)S(1)} %bitcast.127), channel_id=1, source_target_pairs={{0,9},{1,8},{2,11},{3,10},{4,13},{5,12},{6,15},{7,14},{8,1},{9,0},... | collective-permute-start | bytes 1572872 | tf_op jit(solution)/shard_map/ppermute | solution.py:79
  179.0 111.4 %collective-permute-start.9 = (bf16[128,32,2,32]{0,3,2,1:T(8,128)(2,1)S(1)}, bf16[128,32,2,32]{0,3,2,1:T(8,128)(2,1)S(1)}, u32[]{:S(2)}, u32[]{:S(2)}) collective-permute-start(bf16[128,32,2,32]{0,3,2,1:T(8,128)(2,1)S(1)} %bitcast.126), channel_id=1, source_target_pairs={{0,10},{1,11},{2,8},{3,9},{4,14},{5,15},{6,12},{7,13},{8,2},{9,3},... | collective-permute-start | bytes 1572872 | tf_op jit(solution)/shard_map/ppermute | solution.py:79
  212.5 100.7 %collective-permute-start.10 = (bf16[128,32,2,32]{0,3,2,1:T(8,128)(2,1)S(1)}, bf16[128,32,2,32]{0,3,2,1:T(8,128)(2,1)S(1)}, u32[]{:S(2)}, u32[]{:S(2)}) collective-permute-start(bf16[128,32,2,32]{0,3,2,1:T(8,128)(2,1)S(1)} %bitcast.125), channel_id=1, source_target_pairs={{0,11},{1,10},{2,9},{3,8},{4,15},{5,14},{6,13},{7,12},{8,3},{9,2},... | collective-permute-start | bytes 1572872 | tf_op jit(solution)/shard_map/ppermute | solution.py:79
  223.8 90.1 %collective-permute-start.11 = (bf16[128,32,2,32]{0,3,2,1:T(8,128)(2,1)S(1)}, bf16[128,32,2,32]{0,3,2,1:T(8,128)(2,1)S(1)}, u32[]{:S(2)}, u32[]{:S(2)}) collective-permute-start(bf16[128,32,2,32]{0,3,2,1:T(8,128)(2,1)S(1)} %bitcast.124), channel_id=1, source_target_pairs={{0,12},{1,13},{2,14},{3,15},{4,8},{5,9},{6,10},{7,11},{8,4},{9,5},... | collective-permute-start | bytes 1572872 | tf_op jit(solution)/shard_map/ppermute | solution.py:79
  225.9 88.9 %collective-permute-start.12 = (bf16[128,32,2,32]{0,3,2,1:T(8,128)(2,1)S(1)}, bf16[128,32,2,32]{0,3,2,1:T(8,128)(2,1)S(1)}, u32[]{:S(2)}, u32[]{:S(2)}) collective-permute-start(bf16[128,32,2,32]{0,3,2,1:T(8,128)(2,1)S(1)} %bitcast.123), channel_id=1, source_target_pairs={{0,13},{1,12},{2,15},{3,14},{4,9},{5,8},{6,11},{7,10},{8,5},{9,4},... | collective-permute-start | bytes 1572872 | tf_op jit(solution)/shard_map/ppermute | solution.py:79
  229.2 86.4 %collective-permute-start.13 = (bf16[128,32,2,32]{0,3,2,1:T(8,128)(2,1)S(1)}, bf16[128,32,2,32]{0,3,2,1:T(8,128)(2,1)S(1)}, u32[]{:S(2)}, u32[]{:S(2)}) collective-permute-start(bf16[128,32,2,32]{0,3,2,1:T(8,128)(2,1)S(1)} %bitcast.122), channel_id=1, source_target_pairs={{0,14},{1,15},{2,12},{3,13},{4,10},{5,11},{6,8},{7,9},{8,6},{9,7},... | collective-permute-start | bytes 1572872 | tf_op jit(solution)/shard_map/ppermute | solution.py:79
  290.4 26.1 %collective-permute-start.14 = (bf16[128,32,2,32]{0,3,2,1:T(8,128)(2,1)S(1)}, bf16[128,32,2,32]{0,3,2,1:T(8,128)(2,1)S(1)}, u32[]{:S(2)}, u32[]{:S(2)}) collective-permute-start(bf16[128,32,2,32]{0,3,2,1:T(8,128)(2,1)S(1)} %bitcast.121), channel_id=1, source_target_pairs={{0,15},{1,14},{2,13},{3,12},{4,11},{5,10},{6,9},{7,8},{8,7},{9,6},... | collective-permute-start | bytes 1572872 | tf_op jit(solution)/shard_map/ppermute | solution.py:79
  347.1 140.3 %copy-start = (f32[1024]{0:T(1024)S(1)}, f32[1024]{0:T(1024)}, u32[]{:S(2)}) copy-start(f32[1024]{0:T(1024)} %param.10) | copy-start | bytes 12292
  347.2 140.3 %copy-start.1 = (f32[1024]{0:T(1024)S(1)}, f32[1024]{0:T(1024)}, u32[]{:S(2)}) copy-start(f32[1024]{0:T(1024)} %param.9) | copy-start | bytes 12292
  347.2 141.5 %copy-start.2 = (s32[128]{0:T(128)S(1)}, s32[128]{0:T(128)}, u32[]{:S(2)}) copy-start(s32[128]{0:T(128)} %param.7) | copy-start | bytes 1540
Sparse Core Ops, SparseCore 0:
  356.3 131.1 all-reduce.1
